TPU v7x, 128 devices: a whole 4x4x4 slice. The times are simulated.
128 devices in a mesh: slab: 16 (over x_lo, z, core), brick: 8 (over y, x_hi).
Axes of the slice: x: 4 (x_hi: 2, x_lo: 2; x = x_hi * 2 + x_lo), y: 4, z: 4, core: 2. Of those that a mesh axis runs over, the one named last changes fastest.
Arguments:
- features: bfloat16 [64, 262144], P(None, ('slab', 'brick')), may hold values from -6 to 6
- tangents: bfloat16 [4, 64, 262144], P(None, None, ('slab', 'brick')), may hold values from -6 to 6
- route: int32 [262144, 1], P(('slab', 'brick')), may hold values from 0 to 7; in each aligned block of 2048 rows (0 to 2047, 2048 to 4095, ...) at most 512 rows name the same one
- cell_local: int32 [262144], P(('slab', 'brick')), may hold values from 0 to 2047
- stencil: int32 [262144], P(('slab', 'brick')), may hold values from 0 to 7
- stencil_table: float32 [8, 64], replicated, may hold values from -6 to 6
- taps1: float32 [3, 3, 64], replicated, may hold values from -3.5 to 3.5
- taps2: float32 [3, 3, 64], replicated, may hold values from -3.5 to 3.5
- point1: bfloat16 [64, 64], replicated, may hold values from -0.75 to 0.75
- point2: bfloat16 [64, 64], replicated, may hold values from -0.75 to 0.75
- bias1: float32 [64], replicated, may hold values from -3 to 3
- bias2: float32 [64], replicated, may hold values from -3 to 3
- readout: float32 [64], replicated, may hold values from -12 to 12
Outputs:
- hvp: float32 [4, 64, 262144], P(None, None, ('slab', 'brick'))
Inputs may be any that keep to these rules, and one draw needn't show every extreme that they name: `route`: at most 512 of the atoms of one device name one brick, and some device names some brick exactly 512 times.
All inputs are finite; a program needn't handle non-finite values.
Results may differ from a plain program's by a relative error of at most 0.008.
The roundings to bfloat16 on the way count: a program that leaves them out, or rounds other values in their place, can miss the bound.
Values may be sent and summed in bfloat16 or wider, within the bound.
A program may use at most 128 MiB of HBM per device.

v0:
```python
import functools

import jax
import jax.numpy as jnp
from jax import lax
from jax.experimental import pallas as pl
from jax.experimental.pallas import tpu as pltpu
from jax.sharding import PartitionSpec as P

NG = 64
CH = 64
NT = 4
KSETS = 8
BRICKS = 8
SLABS = 16
ATOMS = 2048
CAP = 512
CZ = 4
CY = 8
XH = 32
LANES = 2 * CH
ROWS = CZ * CY * XH
HEAD = 16
GROUPS = ((0, HEAD + CH), (HEAD + CH, 2 * CH), (HEAD + 3 * CH, 2 * CH))
DEPTH = HEAD + (NT + 1) * CH
F32 = jnp.float32
BF16 = jnp.bfloat16
MESH = pl.DeviceIdType.MESH
VMEM = pl.BlockSpec(memory_space=pltpu.VMEM)


def table_rows(stencil_row, table_t):
    out = jnp.broadcast_to(table_t[:, 0:1], (CH, stencil_row.shape[1]))
    for k in range(1, KSETS):
        out = jnp.where(stencil_row == k, table_t[:, k : k + 1], out)
    return out


def pack_kernel(feat, tang, rel, cell, sten, table_t, out, slot_out, data, place, column):
    step = 512
    for c in range(ATOMS // step):
        cols = slice(c * step, (c + 1) * step)
        tab = table_rows(sten[:, cols], table_t[...])
        cells = cell[:, cols]
        high = (cells // NG + 1).astype(F32)
        low = (cells % NG).astype(F32)
        which = lax.broadcasted_iota(jnp.int32, (HEAD, step), 0)
        head = jnp.where(which == 0, high, jnp.where(which == 1, low, 0.0))
        data[0:HEAD, cols] = head.astype(BF16)
        data[HEAD : HEAD + CH, cols] = (feat[:, cols].astype(F32) * tab).astype(BF16)
        for k in range(NT):
            at = HEAD + (k + 1) * CH
            data[at : at + CH, cols] = (tang[k, :, cols].astype(F32) * tab).astype(BF16)
    width = 256
    upper = lax.broadcasted_iota(jnp.int32, (width, width), 0) <= lax.broadcasted_iota(
        jnp.int32, (width, width), 1
    )
    upper = jnp.where(upper, 1.0, 0.0).astype(BF16)
    carry = jnp.zeros((BRICKS, 1), F32)
    for c in range(ATOMS // width):
        cols = slice(c * width, (c + 1) * width)
        dest = rel[:, cols]
        hit = lax.broadcasted_iota(jnp.int32, (BRICKS, width), 0) == dest
        hot = jnp.where(hit, 1.0, 0.0)
        count = jnp.dot(hot.astype(BF16), upper, preferred_element_type=F32) + carry
        position = jnp.sum(jnp.where(hit, count, 0.0), axis=0, keepdims=True) - 1.0
        slot = dest.astype(F32) * CAP + position
        slot_out[:, cols] = slot.astype(jnp.int32)
        column[cols, :] = jnp.transpose(jnp.broadcast_to(slot, (8, width)))
        carry = carry + jnp.sum(hot, axis=1, keepdims=True)

    def one(r, _):
        base = (r * CAP).astype(F32)
        for c in range(ATOMS // 128):
            rows = slice(c * 128, (c + 1) * 128)
            lane = lax.broadcasted_iota(jnp.int32, (128, CAP), 1).astype(F32) + base
            place[rows, :] = jnp.where(column[rows, 0:1] == lane, 1.0, 0.0).astype(BF16)
        out[r] = jnp.dot(data[...], place[...], preferred_element_type=F32).astype(BF16)
        return 0

    lax.fori_loop(0, BRICKS, one, 0)


def unpack_kernel(back, slot, sten, table_t, out):
    width = slot.shape[1]
    acc = jnp.zeros((NT * CH, width), F32)
    for r in range(BRICKS):
        row = lax.broadcasted_iota(jnp.int32, (CAP, width), 0) + r * CAP
        place = jnp.where(row == slot[...], 1.0, 0.0).astype(BF16)
        acc = acc + jnp.dot(back[r], place, preferred_element_type=F32)
    tab = table_rows(sten[...], table_t[...])
    for k in range(NT):
        out[k] = acc[k * CH : (k + 1) * CH] * tab


def owner(brick):
    side = brick // 4
    return 2 * (brick + side * (7 - 2 * brick)) + side


def grid_kernel(
    packed, taps, w1, w1b, w2, w2b, rows3,
    back,
    recv, hot, ext, acc, t_one, slope, bend, curve, final, send,
    a_send, a_recv, h_send, h_recv, b_send, b_recv, own_sem,
):
    slab = lax.axis_index("slab")
    place = lax.axis_index("brick")
    x_hi = place % 2
    y = place // 2
    brick = y + x_hi * (7 - 2 * y)
    s_up, s_down = (slab + 1) % SLABS, (slab + SLABS - 1) % SLABS
    b_up, b_down = owner((brick + 1) % BRICKS), owner((brick + BRICKS - 1) % BRICKS)

    def at(s, b):
        return {"slab": s, "brick": b}

    peers = [at(slab, (place + r) % BRICKS) for r in range(1, BRICKS)]
    around = [
        at(s_down, place), at(s_up, place),
        at(s_down, b_down), at(s_down, b_up), at(s_up, b_down), at(s_up, b_up),
    ]
    gate = pltpu.get_barrier_semaphore()
    for peer in peers + around:
        pl.semaphore_signal(gate, inc=1, device_id=peer, device_id_type=MESH)
    pl.semaphore_wait(gate, len(peers) + len(around))

    def forward(g, r):
        start, size = GROUPS[g]
        return pltpu.make_async_remote_copy(
            src_ref=packed.at[r, pl.ds(start, size)],
            dst_ref=recv.at[r, pl.ds(start, size)],
            send_sem=a_send.at[g, r],
            recv_sem=a_recv.at[g, r],
            device_id=at(slab, (place + r) % BRICKS),
            device_id_type=MESH,
        )

    own = pltpu.make_async_copy(packed.at[0], recv.at[0], own_sem)
    own.start()
    for g in range(len(GROUPS)):
        for r in range(1, BRICKS):
            forward(g, r).start()
    own.wait()

    def halo(stage, v):
        e = stage * (NT + 1) + v
        field = ext.at[e]
        moves = (
            (field.at[1, pl.ds(1, CY)], field.at[CZ + 1, pl.ds(1, CY)], at(s_down, place)),
            (field.at[CZ, pl.ds(1, CY)], field.at[0, pl.ds(1, CY)], at(s_up, place)),
            (field.at[pl.ds(1, CZ), 1], field.at[pl.ds(1, CZ), CY + 1], at(slab, b_down)),
            (field.at[pl.ds(1, CZ), CY], field.at[pl.ds(1, CZ), 0], at(slab, b_up)),
            (field.at[1, 1], field.at[CZ + 1, CY + 1], at(s_down, b_down)),
            (field.at[1, CY], field.at[CZ + 1, 0], at(s_down, b_up)),
            (field.at[CZ, 1], field.at[0, CY + 1], at(s_up, b_down)),
            (field.at[CZ, CY], field.at[0, 0], at(s_up, b_up)),
        )
        return [
            pltpu.make_async_remote_copy(
                src_ref=src,
                dst_ref=dst,
                send_sem=h_send.at[e, i],
                recv_sem=h_recv.at[e, i],
                device_id=to,
                device_id_type=MESH,
            )
            for i, (src, dst, to) in enumerate(moves)
        ]

    def launch(stage, v):
        for copy in halo(stage, v):
            copy.start()

    def arrive(stage, v):
        for copy in halo(stage, v):
            copy.wait_recv()

    def split_mask(r):
        low = recv[r, 0:HEAD, :].astype(F32)[1:2, :]
        return low >= XH

    def make_hot(r):
        head = recv[r, 0:HEAD, :].astype(F32)
        high, low = head[0:1, :], head[1:2, :]
        label = (high - 1.0) * XH + jnp.where(low >= XH, low - XH, low)

        def block(i, _):
            row = (lax.broadcasted_iota(jnp.int32, (128, CAP), 0) + i * 128).astype(F32)
            hot[r, pl.ds(pl.multiple_of(i * 128, 128), 128), :] = jnp.where(
                row == label, 1.0, 0.0
            ).astype(BF16)
            return 0

        lax.fori_loop(0, ROWS // 128, block, 0)

    def deposit(g, first, vectors):
        width = LANES * vectors
        acc[:, 0:width] = jnp.zeros((ROWS, width), F32)

        def source(r, _):
            @pl.when(r > 0)
            def _():
                forward(g, r).wait_recv()

            if g == 0:
                make_hot(r)
            upper = split_mask(r)
            parts = []
            for i in range(vectors):
                rows = HEAD + (first + i) * CH
                value = recv[r, rows : rows + CH, :].astype(F32)
                parts.append(jnp.where(upper, 0.0, value).astype(BF16))
                parts.append(jnp.where(upper, value, 0.0).astype(BF16))
            spread = jnp.concatenate(parts, axis=0)
            acc[:, 0:width] += lax.dot_general(
                hot[r], spread, (((1,), (1,)), ((), ())), preferred_element_type=F32
            )
            return 0

        lax.fori_loop(0, BRICKS, source, 0)
        for i in range(vectors):
            for z in range(CZ):
                part = acc[z * CY * XH : (z + 1) * CY * XH, i * LANES : (i + 1) * LANES]
                ext[first + i, z + 1, 1 : CY + 1] = part.astype(BF16).reshape(CY, XH, LANES)
            launch(0, first + i)

    def convolve(stage, v, z):
        e = stage * (NT + 1) + v

        def weight(axis, tap):
            i = stage * 9 + axis * 3 + tap
            return taps[i : i + 1, :].reshape(1, 1, LANES)

        along = (
            weight(0, 0) * ext[e, z].astype(F32)
            + weight(0, 1) * ext[e, z + 1].astype(F32)
            + weight(0, 2) * ext[e, z + 2].astype(F32)
        )
        across = (
            weight(1, 0) * along[0:CY]
            + weight(1, 1) * along[1 : CY + 1]
            + weight(1, 2) * along[2 : CY + 2]
        )
        flat = across.reshape(CY, XH, LANES)
        sub = lax.broadcasted_iota(jnp.int32, (CY, 8, LANES), 1)
        back_one = pltpu.roll(flat, 1, 1)
        first = back_one[:, 0:8, :]
        first = jnp.where(sub == 0, pltpu.roll(first, CH, 2), first)
        before = jnp.concatenate([first, back_one[:, 8:, :]], axis=1)
        on_one = pltpu.roll(flat, XH - 1, 1)
        last = on_one[:, XH - 8 :, :]
        last = jnp.where(sub == 7, pltpu.roll(last, CH, 2), last)
        after = jnp.concatenate([on_one[:, : XH - 8, :], last], axis=1)
        out = weight(2, 0) * before + weight(2, 1) * flat + weight(2, 2) * after
        return out.reshape(CY * XH, LANES)

    plane = CY * XH

    def span(z):
        return pl.ds(pl.multiple_of(z * plane, plane), plane)

    def mix(value, weights):
        return jnp.dot(value.astype(BF16), weights[...], preferred_element_type=F32)

    def put(stage, v, z, value):
        ext[stage * (NT + 1) + v, z + 1, 1 : CY + 1] = value.astype(BF16).reshape(CY, XH, LANES)

    def planes(body):
        def step(z, _):
            body(z)
            return 0

        lax.fori_loop(0, CZ, step, 0)

    def sweep(stage, body, low, high):
        def step(v, _):
            arrive(stage, v)
            planes(functools.partial(body, v))
            if stage < 3:
                launch(stage + 1, v)
            return 0

        lax.fori_loop(low, high, step, 0)

    def base_one(v, z):
        pre = mix(convolve(0, 0, z), w1) + rows3[0:1, :]
        sg = jax.nn.sigmoid(pre)
        slope[span(z), :] = sg * (1.0 + pre * (1.0 - sg))
        bend[span(z), :] = sg * (1.0 - sg) * (2.0 + pre * (1.0 - 2.0 * sg))
        put(1, 0, z, pre * sg)

    def tangent_one(v, z):
        t = mix(convolve(0, v, z), w1)
        t_one[v - 1, span(z), :] = t
        put(1, v, z, slope[span(z), :] * t)

    def base_two(v, z):
        pre = mix(convolve(1, 0, z), w2) + rows3[1:2, :]
        sg = jax.nn.sigmoid(pre)
        scale = rows3[2:3, :]
        curve[span(z), :] = sg * (1.0 - sg) * (2.0 + pre * (1.0 - 2.0 * sg)) * scale
        put(2, 0, z, mix(sg * (1.0 + pre * (1.0 - sg)) * scale, w2b))

    def tangent_two(v, z):
        dz = mix(convolve(1, v, z), w2)
        put(2, v, z, mix(curve[span(z), :] * dz, w2b))

    def base_three(z):
        bend[span(z), :] = bend[span(z), :] * convolve(2, 0, z)

    def tangent_three(v, z):
        term = bend[span(z), :] * t_one[v - 1, span(z), :] + slope[span(z), :] * convolve(2, v, z)
        put(3, v, z, mix(term, w1b))

    def tangent_four(v, z):
        out = jnp.transpose(convolve(3, v, z)).astype(BF16)
        final[pl.ds(pl.multiple_of((v - 1) * LANES, LANES), LANES), span(z)] = out

    def backward(p, r):
        return pltpu.make_async_remote_copy(
            src_ref=send.at[r, pl.ds(p * LANES, LANES)],
            dst_ref=back.at[r, pl.ds(p * LANES, LANES)],
            send_sem=b_send.at[p, r],
            recv_sem=b_recv.at[p, r],
            device_id=at(slab, (place + BRICKS - r) % BRICKS),
            device_id_type=MESH,
        )

    def pick(p):
        def source(i, _):
            r = BRICKS - 1 - i
            got = jnp.dot(
                final[2 * p * LANES : 2 * (p + 1) * LANES, :], hot[r], preferred_element_type=F32
            )
            upper = split_mask(r)
            parts = []
            for k in range(2):
                at_k = k * LANES
                parts.append(
                    jnp.where(upper, got[at_k + CH : at_k + LANES], got[at_k : at_k + CH])
                )
            chosen = jnp.concatenate(parts, axis=0).astype(BF16)

            @pl.when(r > 0)
            def _():
                send[r, p * LANES : (p + 1) * LANES, :] = chosen
                backward(p, r).start()

            @pl.when(r == 0)
            def _():
                back[0, p * LANES : (p + 1) * LANES, :] = chosen

            return 0

        lax.fori_loop(0, BRICKS, source, 0)

    deposit(0, 0, 1)
    deposit(1, 1, 2)
    sweep(0, base_one, 0, 1)
    deposit(2, 3, 2)
    sweep(0, tangent_one, 1, 3)
    sweep(1, base_two, 0, 1)
    sweep(0, tangent_one, 3, 5)
    sweep(1, tangent_two, 1, 5)
    arrive(2, 0)
    planes(base_three)
    sweep(2, tangent_three, 1, 5)
    sweep(3, tangent_four, 1, 3)
    pick(0)
    sweep(3, tangent_four, 3, 5)
    pick(1)

    def finish(r, _):
        for p in range(2):
            backward(p, r).wait()
        for g in range(len(GROUPS)):
            forward(g, r).wait_send()
        return 0

    lax.fori_loop(1, BRICKS, finish, 0)

    def finish_halo(v, _):
        for stage in range(4):
            if stage == 3:
                @pl.when(v > 0)
                def _():
                    for copy in halo(3, v):
                        copy.wait_send()
            else:
                for copy in halo(stage, v):
                    copy.wait_send()
        return 0

    lax.fori_loop(0, NT + 1, finish_halo, 0)


def shards(
    features, tangents, route, cell_local, stencil, stencil_table,
    taps1, taps2, point1, point2, bias1, bias2, readout,
):
    table_t = stencil_table.T
    rel = (owner(route.reshape(1, ATOMS)) - lax.axis_index("brick") + BRICKS) % BRICKS
    cell = cell_local.reshape(1, ATOMS)
    sten = stencil.reshape(1, ATOMS)
    packed, slot = pl.pallas_call(
        pack_kernel,
        name="pack",
        out_shape=(
            jax.ShapeDtypeStruct((BRICKS, DEPTH, CAP), BF16),
            jax.ShapeDtypeStruct((1, ATOMS), jnp.int32),
        ),
        in_specs=[VMEM] * 6,
        out_specs=(VMEM, VMEM),
        scratch_shapes=[
            pltpu.VMEM((DEPTH, ATOMS), BF16),
            pltpu.VMEM((ATOMS, CAP), BF16),
            pltpu.VMEM((ATOMS, 8), F32),
        ],
    )(features, tangents, rel, cell, sten, table_t)

    def doubled(rows):
        return jnp.concatenate([rows, rows], axis=-1)

    forward_taps = [taps1.reshape(9, CH), taps2.reshape(9, CH)]
    flipped = [taps2[:, ::-1].reshape(9, CH), taps1[:, ::-1].reshape(9, CH)]
    taps = doubled(jnp.concatenate(forward_taps + flipped, axis=0))
    rows3 = doubled(jnp.stack([bias1, bias2, readout]))

    def block(w):
        zero = jnp.zeros_like(w)
        return jnp.concatenate(
            [jnp.concatenate([w, zero], axis=1), jnp.concatenate([zero, w], axis=1)], axis=0
        )

    fields = 4 * (NT + 1)
    dma = pltpu.SemaphoreType.DMA
    back = pl.pallas_call(
        grid_kernel,
        name="grid",
        out_shape=jax.ShapeDtypeStruct((BRICKS, NT * CH, CAP), BF16),
        in_specs=[VMEM] * 7,
        out_specs=VMEM,
        scratch_shapes=[
            pltpu.VMEM((BRICKS, DEPTH, CAP), BF16),
            pltpu.VMEM((BRICKS, ROWS, CAP), BF16),
            pltpu.VMEM((fields, CZ + 2, CY + 2, XH, LANES), BF16),
            pltpu.VMEM((ROWS, 2 * LANES), F32),
            pltpu.VMEM((NT, ROWS, LANES), F32),
            pltpu.VMEM((ROWS, LANES), F32),
            pltpu.VMEM((ROWS, LANES), F32),
            pltpu.VMEM((ROWS, LANES), F32),
            pltpu.VMEM((NT * LANES, ROWS), BF16),
            pltpu.VMEM((BRICKS, NT * CH, CAP), BF16),
            dma((3, BRICKS)),
            dma((3, BRICKS)),
            dma((fields, 8)),
            dma((fields, 8)),
            dma((2, BRICKS)),
            dma((2, BRICKS)),
            dma,
        ],
        compiler_params=pltpu.CompilerParams(
            collective_id=0, has_side_effects=True, vmem_limit_bytes=60 * 1024 * 1024
        ),
    )(packed, taps, block(point1.T), block(point1), block(point2.T), block(point2), rows3)
    width = 512
    return pl.pallas_call(
        unpack_kernel,
        name="unpack",
        grid=(ATOMS // width,),
        out_shape=jax.ShapeDtypeStruct((NT, CH, ATOMS), F32),
        in_specs=[
            pl.BlockSpec((BRICKS, NT * CH, CAP), lambda i: (0, 0, 0)),
            pl.BlockSpec((1, width), lambda i: (0, i)),
            pl.BlockSpec((1, width), lambda i: (0, i)),
            pl.BlockSpec((CH, KSETS), lambda i: (0, 0)),
        ],
        out_specs=pl.BlockSpec((NT, CH, width), lambda i: (0, 0, i)),
    )(back, slot, sten, table_t)


def solution(mesh):
    placed = (
        P(None, ("slab", "brick")),
        P(None, None, ("slab", "brick")),
        P(("slab", "brick"), None),
        P(("slab", "brick")),
        P(("slab", "brick")),
        P(),
        P(),
        P(),
        P(),
        P(),
        P(),
        P(),
        P(),
    )
    return jax.shard_map(
        shards,
        mesh=mesh,
        in_specs=placed,
        out_specs=P(None, None, ("slab", "brick")),
        check_vma=False,
    )
```

profile of v0, /device:TPU:17, one launch (start us, length us, event | category | flops | bytes accessed | tf_op | source)
XLA Modules:
  0.0 139.7 jit_solution(204036362236196231)
XLA Ops:
  0.0 1.4 maximum_maximum_fusion.1.rows3
  1.4 0.7 rev.7
  2.1 0.7 rev.6
  2.8 1.4 and_select_fusion.rel
  4.2 0.7 reshape.212
  4.9 0.7 reshape.213
  5.6 0.7 maximum_maximum_fusion.taps
  6.3 0.8 copy.15
  7.1 0.8 copy.16
  7.9 1.4 copy.14
  9.3 1.5 %fusion.10 = (bf16[128,128]{1,0:T(8,128)(2,1)}, bf16[128,128]{1,0:T(8,128)(2,1)}) fusion(bf16[64,64]{1,0:T(8,128)(2,1)S(1)} %bitcast.35, bf16[64,64]{1,0:T(8,128)(2,1)} %param.22), kind=kLoop, calls=%fused_computation.14 | loop fusion | flops 229376 | bytes 81920 | tf_op jit(solution)/shard_map/concatenate | solution.py:432
  10.8 1.5 %fusion.8 = (bf16[128,128]{1,0:T(8,128)(2,1)}, bf16[128,128]{1,0:T(8,128)(2,1)}) fusion(bf16[64,64]{1,0:T(8,128)(2,1)S(1)} %bitcast.34, bf16[64,64]{1,0:T(8,128)(2,1)} %param.21), kind=kLoop, calls=%fused_computation.12 | loop fusion | flops 229376 | bytes 81920 | tf_op jit(solution)/shard_map/concatenate | solution.py:432
  12.3 11.4 %pack.1 = (bf16[8,336,512]{2,1,0:T(8,128)(2,1)}, s32[1,2048]{1,0:T(1,128)}) custom-call(bf16[64,2048]{1,0:T(8,128)(2,1)} %feat.1, bf16[4,64,2048]{2,1,0:T(8,128)(2,1)} %tang.1, s32[1,2048]{1,0:T(1,128)} %and_select_fusion.rel, s32[1,2048]{1,0:T(1,128)} %bitcast.38, s32[1,2048]{1,0:T(1,128)} %bitcast.36, f32[64,8]{1,0:T(8,128)} %bitcast.32), custom_call_target="tpu_custom_call" | custom-call | tf_op jit(solution)/shard_map/pack/pallas_call | solution.py:406
  23.8 108.4 %grid.1.back = bf16[8,256,512]{2,1,0:T(8,128)(2,1)} custom-call(bf16[8,336,512]{2,1,0:T(8,128)(2,1)} %get-tuple-element.7.packed, f32[36,128]{1,0:T(8,128)} %maximum_maximum_fusion.taps, bf16[128,128]{1,0:T(8,128)(2,1)} %get-tuple-element.9.w1, bf16[128,128]{1,0:T(8,128)(2,1)} %get-tuple-element.10.w1b, bf16[128,128]{1,0:T(8,128)(2,1)} %get-tuple-element.11.w2, ...), custom_call_target="tpu_custom_call" | custom-call | tf_op jit(solution)/shard_map/grid/pallas_call | solution.py:438
  132.2 7.6 %unpack.1 = f32[4,64,2048]{2,1,0:T(8,128)} custom-call(bf16[8,256,512]{2,1,0:T(8,128)(2,1)} %grid.1.back, s32[1,2048]{1,0:T(1,128)} %get-tuple-element.8.slot, s32[1,2048]{1,0:T(1,128)} %bitcast.37, f32[64,8]{1,0:T(8,128)} %bitcast.33), custom_call_target="tpu_custom_call" | custom-call | tf_op jit(solution)/shard_map/unpack/pallas_call | solution.py:468
  (2 shorter events, 0.0 us)
where the time goes:
time: 141 us; the launch traced here: 140 us
  Pallas kernels  127 us (90%)
  other arithmetic  6.46 us (5%)
  local copies, waits for them, and re-layouts  5.85 us (4%)
    pallas_call x1, Pallas kernels, shards(): pl.pallas_call(grid_kernel, name='grid', out_shape=jax.ShapeDtypeStruct((...  108 us
    pallas_call x1, Pallas kernels, shards(): pl.pallas_call(pack_kernel, name='pack', out_shape=(jax.ShapeDtypeStruct(...  11.4 us
    pallas_call x1, Pallas kernels, shards(): pl.pallas_call(unpack_kernel, name='unpack', grid=(ATOMS // width,), out_...  7.58 us
    unnamed x3, local copies, waits for them, and re-layouts  3 us
    concatenate x2, other arithmetic, block(): jnp.concatenate([jnp.concatenate([w, zero], axis=1), jnp.concatenate([zer...  3 us

commit v1 on v0

--- a/solution.py
+++ b/solution.py
@@ -29,80 +29,21 @@
 VMEM = pl.BlockSpec(memory_space=pltpu.VMEM)
 
 
-def table_rows(stencil_row, table_t):
-    out = jnp.broadcast_to(table_t[:, 0:1], (CH, stencil_row.shape[1]))
-    for k in range(1, KSETS):
-        out = jnp.where(stencil_row == k, table_t[:, k : k + 1], out)
-    return out
-
-
-def pack_kernel(feat, tang, rel, cell, sten, table_t, out, slot_out, data, place, column):
-    step = 512
-    for c in range(ATOMS // step):
-        cols = slice(c * step, (c + 1) * step)
-        tab = table_rows(sten[:, cols], table_t[...])
-        cells = cell[:, cols]
-        high = (cells // NG + 1).astype(F32)
-        low = (cells % NG).astype(F32)
-        which = lax.broadcasted_iota(jnp.int32, (HEAD, step), 0)
-        head = jnp.where(which == 0, high, jnp.where(which == 1, low, 0.0))
-        data[0:HEAD, cols] = head.astype(BF16)
-        data[HEAD : HEAD + CH, cols] = (feat[:, cols].astype(F32) * tab).astype(BF16)
-        for k in range(NT):
-            at = HEAD + (k + 1) * CH
-            data[at : at + CH, cols] = (tang[k, :, cols].astype(F32) * tab).astype(BF16)
-    width = 256
-    upper = lax.broadcasted_iota(jnp.int32, (width, width), 0) <= lax.broadcasted_iota(
-        jnp.int32, (width, width), 1
-    )
-    upper = jnp.where(upper, 1.0, 0.0).astype(BF16)
-    carry = jnp.zeros((BRICKS, 1), F32)
-    for c in range(ATOMS // width):
-        cols = slice(c * width, (c + 1) * width)
-        dest = rel[:, cols]
-        hit = lax.broadcasted_iota(jnp.int32, (BRICKS, width), 0) == dest
-        hot = jnp.where(hit, 1.0, 0.0)
-        count = jnp.dot(hot.astype(BF16), upper, preferred_element_type=F32) + carry
-        position = jnp.sum(jnp.where(hit, count, 0.0), axis=0, keepdims=True) - 1.0
-        slot = dest.astype(F32) * CAP + position
-        slot_out[:, cols] = slot.astype(jnp.int32)
-        column[cols, :] = jnp.transpose(jnp.broadcast_to(slot, (8, width)))
-        carry = carry + jnp.sum(hot, axis=1, keepdims=True)
-
-    def one(r, _):
-        base = (r * CAP).astype(F32)
-        for c in range(ATOMS // 128):
-            rows = slice(c * 128, (c + 1) * 128)
-            lane = lax.broadcasted_iota(jnp.int32, (128, CAP), 1).astype(F32) + base
-            place[rows, :] = jnp.where(column[rows, 0:1] == lane, 1.0, 0.0).astype(BF16)
-        out[r] = jnp.dot(data[...], place[...], preferred_element_type=F32).astype(BF16)
-        return 0
-
-    lax.fori_loop(0, BRICKS, one, 0)
-
-
-def unpack_kernel(back, slot, sten, table_t, out):
-    width = slot.shape[1]
-    acc = jnp.zeros((NT * CH, width), F32)
-    for r in range(BRICKS):
-        row = lax.broadcasted_iota(jnp.int32, (CAP, width), 0) + r * CAP
-        place = jnp.where(row == slot[...], 1.0, 0.0).astype(BF16)
-        acc = acc + jnp.dot(back[r], place, preferred_element_type=F32)
-    tab = table_rows(sten[...], table_t[...])
-    for k in range(NT):
-        out[k] = acc[k * CH : (k + 1) * CH] * tab
-
-
 def owner(brick):
     side = brick // 4
     return 2 * (brick + side * (7 - 2 * brick)) + side
 
 
-def grid_kernel(
-    packed, taps, w1, w1b, w2, w2b, rows3,
-    back,
-    recv, hot, ext, acc, t_one, slope, bend, curve, final, send,
-    a_send, a_recv, h_send, h_recv, b_send, b_recv, own_sem,
+def twice(value):
+    return jnp.concatenate([value, value], axis=-1)
+
+
+def whole_kernel(
+    feat, tang, route, cell, sten, table, taps_one, taps_two, point_one, point_two, bias_one, bias_two, readout,
+    picked, tab,
+    data, place_in, place_out, column, slots, packed, recv, hot, ext, acc, t_one, slope, bend, curve,
+    final, send, got, total, taps, mixers, rows3,
+    a_send, a_recv, h_send, h_recv, b_send, b_recv,
 ):
     slab = lax.axis_index("slab")
     place = lax.axis_index("brick")
@@ -123,7 +64,6 @@
     gate = pltpu.get_barrier_semaphore()
     for peer in peers + around:
         pl.semaphore_signal(gate, inc=1, device_id=peer, device_id_type=MESH)
-    pl.semaphore_wait(gate, len(peers) + len(around))
 
     def forward(g, r):
         start, size = GROUPS[g]
@@ -136,12 +76,78 @@
             device_id_type=MESH,
         )
 
-    own = pltpu.make_async_copy(packed.at[0], recv.at[0], own_sem)
-    own.start()
-    for g in range(len(GROUPS)):
-        for r in range(1, BRICKS):
-            forward(g, r).start()
-    own.wait()
+    def prepare():
+        table_t = jnp.transpose(twice(table[...]))
+        step = 512
+        for c in range(ATOMS // step):
+            cols = slice(c * step, (c + 1) * step)
+            chosen = jnp.broadcast_to(table_t[0:CH, 0:1], (CH, step))
+            for k in range(1, KSETS):
+                chosen = jnp.where(sten[:, cols] == k, table_t[0:CH, k : k + 1], chosen)
+            tab[:, cols] = chosen
+            cells = cell[:, cols]
+            high = (cells // NG + 1).astype(F32)
+            low = (cells % NG).astype(F32)
+            which = lax.broadcasted_iota(jnp.int32, (HEAD, step), 0)
+            head = jnp.where(which == 0, high, jnp.where(which == 1, low, 0.0))
+            data[0:HEAD, cols] = head.astype(BF16)
+            data[HEAD : HEAD + CH, cols] = (feat[:, cols].astype(F32) * chosen).astype(BF16)
+            for k in range(NT):
+                start = HEAD + (k + 1) * CH
+                data[start : start + CH, cols] = (tang[k, :, cols].astype(F32) * chosen).astype(BF16)
+        width = 256
+        upper = lax.broadcasted_iota(jnp.int32, (width, width), 0) <= lax.broadcasted_iota(
+            jnp.int32, (width, width), 1
+        )
+        upper = jnp.where(upper, 1.0, 0.0).astype(BF16)
+        carry = jnp.zeros((BRICKS, 1), F32)
+        for c in range(ATOMS // width):
+            cols = slice(c * width, (c + 1) * width)
+            dest = (owner(route[:, cols]) - place + BRICKS) % BRICKS
+            hit = lax.broadcasted_iota(jnp.int32, (BRICKS, width), 0) == dest
+            one = jnp.where(hit, 1.0, 0.0)
+            count = jnp.dot(one.astype(BF16), upper, preferred_element_type=F32) + carry
+            position = jnp.sum(jnp.where(hit, count, 0.0), axis=0, keepdims=True) - 1.0
+            slot = jnp.broadcast_to(dest.astype(F32) * CAP + position, (8, width))
+            slots[:, cols] = slot
+            column[cols, :] = jnp.transpose(slot)
+            carry = carry + jnp.sum(one, axis=1, keepdims=True)
+        for stage, (source, flip) in enumerate(
+            ((taps_one, False), (taps_two, False), (taps_two, True), (taps_one, True))
+        ):
+            for axis in range(3):
+                for tap in range(3):
+                    i = stage * 9 + axis * 3 + tap
+                    j = 2 - tap if flip else tap
+                    taps[i : i + 1, :] = twice(source[axis, j : j + 1, :])
+        rows3[0:1, :] = twice(bias_one[...])
+        rows3[1:2, :] = twice(bias_two[...])
+        rows3[2:3, :] = twice(readout[...])
+        for i, point in enumerate((point_one, point_two)):
+            value = point[...].astype(F32)
+            zero = jnp.zeros_like(value)
+            mixers[i, 0:CH, :] = jnp.concatenate([value, zero], axis=1).astype(BF16)
+            mixers[i, CH:LANES, :] = jnp.concatenate([zero, value], axis=1).astype(BF16)
+
+    def pack(r):
+        base = r * CAP
+        for c in range(ATOMS // 128):
+            rows = slice(c * 128, (c + 1) * 128)
+            lane = (lax.broadcasted_iota(jnp.int32, (128, CAP), 1) + base).astype(F32)
+            place_in[rows, :] = jnp.where(column[rows, 0:1] == lane, 1.0, 0.0).astype(BF16)
+        return jnp.dot(data[...], place_in[...], preferred_element_type=F32).astype(BF16)
+
+    def unpack(p, r):
+        def block(i, _):
+            row = (lax.broadcasted_iota(jnp.int32, (64, ATOMS), 0) + (i * 64 + r * CAP)).astype(F32)
+            place_out[pl.ds(pl.multiple_of(i * 64, 64), 64), :] = jnp.where(
+                row == slots[0:1, :], 1.0, 0.0
+            ).astype(BF16)
+            return 0
+
+        lax.fori_loop(0, CAP // 64, block, 0)
+        rows = slice(p * LANES, (p + 1) * LANES)
+        total[rows, :] += jnp.dot(got[r, rows, :], place_out[...], preferred_element_type=F32)
 
     def halo(stage, v):
         e = stage * (NT + 1) + v
@@ -258,20 +264,20 @@
     plane = CY * XH
 
     def span(z):
-        return pl.ds(pl.multiple_of(z * plane, plane), plane)
-
-    def mix(value, weights):
-        return jnp.dot(value.astype(BF16), weights[...], preferred_element_type=F32)
+        return slice(z * plane, (z + 1) * plane)
+
+    def mix(value, i, back):
+        sides = ((1,), (0,)) if back else ((1,), (1,))
+        return lax.dot_general(
+            value.astype(BF16), mixers[i], (sides, ((), ())), preferred_element_type=F32
+        )
 
     def put(stage, v, z, value):
         ext[stage * (NT + 1) + v, z + 1, 1 : CY + 1] = value.astype(BF16).reshape(CY, XH, LANES)
 
     def planes(body):
-        def step(z, _):
+        for z in range(CZ):
             body(z)
-            return 0
-
-        lax.fori_loop(0, CZ, step, 0)
 
     def sweep(stage, body, low, high):
         def step(v, _):
@@ -284,34 +290,34 @@
         lax.fori_loop(low, high, step, 0)
 
     def base_one(v, z):
-        pre = mix(convolve(0, 0, z), w1) + rows3[0:1, :]
+        pre = mix(convolve(0, 0, z), 0, False) + rows3[0:1, :]
         sg = jax.nn.sigmoid(pre)
         slope[span(z), :] = sg * (1.0 + pre * (1.0 - sg))
         bend[span(z), :] = sg * (1.0 - sg) * (2.0 + pre * (1.0 - 2.0 * sg))
         put(1, 0, z, pre * sg)
 
     def tangent_one(v, z):
-        t = mix(convolve(0, v, z), w1)
+        t = mix(convolve(0, v, z), 0, False)
         t_one[v - 1, span(z), :] = t
         put(1, v, z, slope[span(z), :] * t)
 
     def base_two(v, z):
-        pre = mix(convolve(1, 0, z), w2) + rows3[1:2, :]
+        pre = mix(convolve(1, 0, z), 1, False) + rows3[1:2, :]
         sg = jax.nn.sigmoid(pre)
         scale = rows3[2:3, :]
         curve[span(z), :] = sg * (1.0 - sg) * (2.0 + pre * (1.0 - 2.0 * sg)) * scale
-        put(2, 0, z, mix(sg * (1.0 + pre * (1.0 - sg)) * scale, w2b))
+        put(2, 0, z, mix(sg * (1.0 + pre * (1.0 - sg)) * scale, 1, True))
 
     def tangent_two(v, z):
-        dz = mix(convolve(1, v, z), w2)
-        put(2, v, z, mix(curve[span(z), :] * dz, w2b))
+        dz = mix(convolve(1, v, z), 1, False)
+        put(2, v, z, mix(curve[span(z), :] * dz, 1, True))
 
     def base_three(z):
         bend[span(z), :] = bend[span(z), :] * convolve(2, 0, z)
 
     def tangent_three(v, z):
         term = bend[span(z), :] * t_one[v - 1, span(z), :] + slope[span(z), :] * convolve(2, v, z)
-        put(3, v, z, mix(term, w1b))
+        put(3, v, z, mix(term, 0, True))
 
     def tangent_four(v, z):
         out = jnp.transpose(convolve(3, v, z)).astype(BF16)
@@ -320,7 +326,7 @@
     def backward(p, r):
         return pltpu.make_async_remote_copy(
             src_ref=send.at[r, pl.ds(p * LANES, LANES)],
-            dst_ref=back.at[r, pl.ds(p * LANES, LANES)],
+            dst_ref=got.at[r, pl.ds(p * LANES, LANES)],
             send_sem=b_send.at[p, r],
             recv_sem=b_recv.at[p, r],
             device_id=at(slab, (place + BRICKS - r) % BRICKS),
@@ -330,7 +336,7 @@
     def pick(p):
         def source(i, _):
             r = BRICKS - 1 - i
-            got = jnp.dot(
+            fetched = jnp.dot(
                 final[2 * p * LANES : 2 * (p + 1) * LANES, :], hot[r], preferred_element_type=F32
             )
             upper = split_mask(r)
@@ -338,7 +344,7 @@
             for k in range(2):
                 at_k = k * LANES
                 parts.append(
-                    jnp.where(upper, got[at_k + CH : at_k + LANES], got[at_k : at_k + CH])
+                    jnp.where(upper, fetched[at_k + CH : at_k + LANES], fetched[at_k : at_k + CH])
                 )
             chosen = jnp.concatenate(parts, axis=0).astype(BF16)
 
@@ -349,31 +355,57 @@
 
             @pl.when(r == 0)
             def _():
-                back[0, p * LANES : (p + 1) * LANES, :] = chosen
+                got[0, p * LANES : (p + 1) * LANES, :] = chosen
 
             return 0
 
         lax.fori_loop(0, BRICKS, source, 0)
 
+    prepare()
+    recv[0] = pack(0)
+    pl.semaphore_wait(gate, len(peers) + len(around))
+
+    def pack_and_send(r, _):
+        packed[r] = pack(r)
+        forward(0, r).start()
+        return 0
+
+    lax.fori_loop(1, BRICKS, pack_and_send, 0)
+    for g in range(1, len(GROUPS)):
+        for r in range(1, BRICKS):
+            forward(g, r).start()
     deposit(0, 0, 1)
-    deposit(1, 1, 2)
     sweep(0, base_one, 0, 1)
-    deposit(2, 3, 2)
-    sweep(0, tangent_one, 1, 3)
     sweep(1, base_two, 0, 1)
-    sweep(0, tangent_one, 3, 5)
-    sweep(1, tangent_two, 1, 5)
     arrive(2, 0)
     planes(base_three)
-    sweep(2, tangent_three, 1, 5)
+    deposit(1, 1, 2)
+    sweep(0, tangent_one, 1, 3)
+    sweep(1, tangent_two, 1, 3)
+    deposit(2, 3, 2)
+    sweep(2, tangent_three, 1, 3)
+    sweep(0, tangent_one, 3, 5)
     sweep(3, tangent_four, 1, 3)
     pick(0)
+    sweep(1, tangent_two, 3, 5)
+    sweep(2, tangent_three, 3, 5)
     sweep(3, tangent_four, 3, 5)
     pick(1)
+    total[...] = jnp.zeros_like(total)
+    for p in range(2):
+        unpack(p, 0)
+
+        def collect(r, _):
+            backward(p, r).wait_recv()
+            unpack(p, r)
+            return 0
+
+        lax.fori_loop(1, BRICKS, collect, 0)
+    picked[...] = total[...].astype(BF16)
 
     def finish(r, _):
         for p in range(2):
-            backward(p, r).wait()
+            backward(p, r).wait_send()
         for g in range(len(GROUPS)):
             forward(g, r).wait_send()
         return 0
@@ -399,49 +431,24 @@
     features, tangents, route, cell_local, stencil, stencil_table,
     taps1, taps2, point1, point2, bias1, bias2, readout,
 ):
-    table_t = stencil_table.T
-    rel = (owner(route.reshape(1, ATOMS)) - lax.axis_index("brick") + BRICKS) % BRICKS
-    cell = cell_local.reshape(1, ATOMS)
-    sten = stencil.reshape(1, ATOMS)
-    packed, slot = pl.pallas_call(
-        pack_kernel,
-        name="pack",
+    fields = 4 * (NT + 1)
+    dma = pltpu.SemaphoreType.DMA
+    picked, tab = pl.pallas_call(
+        whole_kernel,
+        name="whole",
         out_shape=(
-            jax.ShapeDtypeStruct((BRICKS, DEPTH, CAP), BF16),
-            jax.ShapeDtypeStruct((1, ATOMS), jnp.int32),
+            jax.ShapeDtypeStruct((NT * CH, ATOMS), BF16),
+            jax.ShapeDtypeStruct((CH, ATOMS), F32),
         ),
-        in_specs=[VMEM] * 6,
+        in_specs=[VMEM] * 13,
         out_specs=(VMEM, VMEM),
         scratch_shapes=[
             pltpu.VMEM((DEPTH, ATOMS), BF16),
             pltpu.VMEM((ATOMS, CAP), BF16),
+            pltpu.VMEM((CAP, ATOMS), BF16),
             pltpu.VMEM((ATOMS, 8), F32),
-        ],
-    )(features, tangents, rel, cell, sten, table_t)
-
-    def doubled(rows):
-        return jnp.concatenate([rows, rows], axis=-1)
-
-    forward_taps = [taps1.reshape(9, CH), taps2.reshape(9, CH)]
-    flipped = [taps2[:, ::-1].reshape(9, CH), taps1[:, ::-1].reshape(9, CH)]
-    taps = doubled(jnp.concatenate(forward_taps + flipped, axis=0))
-    rows3 = doubled(jnp.stack([bias1, bias2, readout]))
-
-    def block(w):
-        zero = jnp.zeros_like(w)
-        return jnp.concatenate(
-            [jnp.concatenate([w, zero], axis=1), jnp.concatenate([zero, w], axis=1)], axis=0
-        )
-
-    fields = 4 * (NT + 1)
-    dma = pltpu.SemaphoreType.DMA
-    back = pl.pallas_call(
-        grid_kernel,
-        name="grid",
-        out_shape=jax.ShapeDtypeStruct((BRICKS, NT * CH, CAP), BF16),
-        in_specs=[VMEM] * 7,
-        out_specs=VMEM,
-        scratch_shapes=[
+            pltpu.VMEM((8, ATOMS), F32),
+            pltpu.VMEM((BRICKS, DEPTH, CAP), BF16),
             pltpu.VMEM((BRICKS, DEPTH, CAP), BF16),
             pltpu.VMEM((BRICKS, ROWS, CAP), BF16),
             pltpu.VMEM((fields, CZ + 2, CY + 2, XH, LANES), BF16),
@@ -452,32 +459,27 @@
             pltpu.VMEM((ROWS, LANES), F32),
             pltpu.VMEM((NT * LANES, ROWS), BF16),
             pltpu.VMEM((BRICKS, NT * CH, CAP), BF16),
+            pltpu.VMEM((BRICKS, NT * CH, CAP), BF16),
+            pltpu.VMEM((NT * CH, ATOMS), F32),
+            pltpu.VMEM((40, LANES), F32),
+            pltpu.VMEM((2, LANES, LANES), BF16),
+            pltpu.VMEM((8, LANES), F32),
             dma((3, BRICKS)),
             dma((3, BRICKS)),
             dma((fields, 8)),
             dma((fields, 8)),
             dma((2, BRICKS)),
             dma((2, BRICKS)),
-            dma,
         ],
         compiler_params=pltpu.CompilerParams(
             collective_id=0, has_side_effects=True, vmem_limit_bytes=60 * 1024 * 1024
         ),
-    )(packed, taps, block(point1.T), block(point1), block(point2.T), block(point2), rows3)
-    width = 512
-    return pl.pallas_call(
-        unpack_kernel,
-        name="unpack",
-        grid=(ATOMS // width,),
-        out_shape=jax.ShapeDtypeStruct((NT, CH, ATOMS), F32),
-        in_specs=[
-            pl.BlockSpec((BRICKS, NT * CH, CAP), lambda i: (0, 0, 0)),
-            pl.BlockSpec((1, width), lambda i: (0, i)),
-            pl.BlockSpec((1, width), lambda i: (0, i)),
-            pl.BlockSpec((CH, KSETS), lambda i: (0, 0)),
-        ],
-        out_specs=pl.BlockSpec((NT, CH, width), lambda i: (0, 0, i)),
-    )(back, slot, sten, table_t)
+    )(
+        features, tangents, route.reshape(1, ATOMS), cell_local.reshape(1, ATOMS), stencil.reshape(1, ATOMS),
+        stencil_table, taps1, taps2, point1, point2,
+        bias1.reshape(1, CH), bias2.reshape(1, CH), readout.reshape(1, CH),
+    )
+    return picked.reshape(NT, CH, ATOMS).astype(F32) * tab
 
 
 def solution(mesh):

time: 141 us -> 144 us (1.021)
  the two profiles are of different devices: /device:TPU:17 before, /device:TPU:0 now
where the time goes in v1:
time: 144 us; the launch traced here: 141 us
  Pallas kernels  138 us (96%)
  other arithmetic  2.93 us (2%)
    pallas_call x1, Pallas kernels, shards(): pl.pallas_call(whole_kernel, name='whole', out_shape=(jax.ShapeDtypeStruc...  138 us
    mul x1, other arithmetic, shards(): return picked.reshape(NT, CH, ATOMS).astype(F32) * tab  2.93 us

profile of v1, /device:TPU:0, one launch (start us, length us, event | category | flops | bytes accessed | tf_op | source)
XLA Modules:
  0.0 141.1 jit_solution(15522701122999753231)
XLA Ops:
  0.0 138.2 %whole.1 = (bf16[256,2048]{1,0:T(8,128)(2,1)}, f32[64,2048]{1,0:T(8,128)}) custom-call(bf16[64,2048]{1,0:T(8,128)(2,1)} %feat.1, bf16[4,64,2048]{2,1,0:T(8,128)(2,1)} %tang.1, s32[1,2048]{1,0:T(1,128)} %bitcast.9, s32[1,2048]{1,0:T(1,128)} %bitcast.10, s32[1,2048]{1,0:T(1,128)} %bitcast.11, f32[8,64]{1,0:T(8,128)} %table.1, f32[3,3,64]{2,1,0:T(4,128)} %taps_one.1, ...), custom_call_target="tpu_custom_call" | custom-call | tf_op jit(solution)/shard_map/whole/pallas_call | solution.py:436
  138.2 2.9 %convert_multiply_fusion = f32[4,64,2048]{2,1,0:T(8,128)} fusion(bf16[4,64,2048]{2,1,0:T(8,128)(2,1)} %bitcast.8, f32[64,2048]{1,0:T(8,128)} %get-tuple-element.8), kind=kLoop, calls=%fused_computation | loop fusion | flops 1048576 | bytes 3670016 | tf_op jit(solution)/shard_map/mul | solution.py:482

commit v2 on v1

--- a/solution.py
+++ b/solution.py
@@ -21,7 +21,7 @@
 LANES = 2 * CH
 ROWS = CZ * CY * XH
 HEAD = 16
-GROUPS = ((0, HEAD + CH), (HEAD + CH, 2 * CH), (HEAD + 3 * CH, 2 * CH))
+GROUPS = ((HEAD, 3 * CH), (HEAD + 3 * CH, 2 * CH), (0, HEAD))
 DEPTH = HEAD + (NT + 1) * CH
 F32 = jnp.float32
 BF16 = jnp.bfloat16
@@ -137,7 +137,7 @@
             place_in[rows, :] = jnp.where(column[rows, 0:1] == lane, 1.0, 0.0).astype(BF16)
         return jnp.dot(data[...], place_in[...], preferred_element_type=F32).astype(BF16)
 
-    def unpack(p, r):
+    def unpack(r):
         def block(i, _):
             row = (lax.broadcasted_iota(jnp.int32, (64, ATOMS), 0) + (i * 64 + r * CAP)).astype(F32)
             place_out[pl.ds(pl.multiple_of(i * 64, 64), 64), :] = jnp.where(
@@ -146,21 +146,20 @@
             return 0
 
         lax.fori_loop(0, CAP // 64, block, 0)
-        rows = slice(p * LANES, (p + 1) * LANES)
-        total[rows, :] += jnp.dot(got[r, rows, :], place_out[...], preferred_element_type=F32)
+        return jnp.dot(got[r], place_out[...], preferred_element_type=F32)
 
     def halo(stage, v):
         e = stage * (NT + 1) + v
         field = ext.at[e]
         moves = (
-            (field.at[1, pl.ds(1, CY)], field.at[CZ + 1, pl.ds(1, CY)], at(s_down, place)),
-            (field.at[CZ, pl.ds(1, CY)], field.at[0, pl.ds(1, CY)], at(s_up, place)),
-            (field.at[pl.ds(1, CZ), 1], field.at[pl.ds(1, CZ), CY + 1], at(slab, b_down)),
-            (field.at[pl.ds(1, CZ), CY], field.at[pl.ds(1, CZ), 0], at(slab, b_up)),
             (field.at[1, 1], field.at[CZ + 1, CY + 1], at(s_down, b_down)),
             (field.at[1, CY], field.at[CZ + 1, 0], at(s_down, b_up)),
             (field.at[CZ, 1], field.at[0, CY + 1], at(s_up, b_down)),
             (field.at[CZ, CY], field.at[0, 0], at(s_up, b_up)),
+            (field.at[pl.ds(1, CZ), 1], field.at[pl.ds(1, CZ), CY + 1], at(slab, b_down)),
+            (field.at[pl.ds(1, CZ), CY], field.at[pl.ds(1, CZ), 0], at(slab, b_up)),
+            (field.at[1, pl.ds(1, CY)], field.at[CZ + 1, pl.ds(1, CY)], at(s_down, place)),
+            (field.at[CZ, pl.ds(1, CY)], field.at[0, pl.ds(1, CY)], at(s_up, place)),
         )
         return [
             pltpu.make_async_remote_copy(
@@ -200,17 +199,13 @@
 
         lax.fori_loop(0, ROWS // 128, block, 0)
 
-    def deposit(g, first, vectors):
+    def deposit(g, low, high):
+        vectors, first = (3, 0) if g == 0 else (2, 3)
         width = LANES * vectors
-        acc[:, 0:width] = jnp.zeros((ROWS, width), F32)
 
         def source(r, _):
-            @pl.when(r > 0)
-            def _():
+            if low > 0:
                 forward(g, r).wait_recv()
-
-            if g == 0:
-                make_hot(r)
             upper = split_mask(r)
             parts = []
             for i in range(vectors):
@@ -219,17 +214,29 @@
                 parts.append(jnp.where(upper, 0.0, value).astype(BF16))
                 parts.append(jnp.where(upper, value, 0.0).astype(BF16))
             spread = jnp.concatenate(parts, axis=0)
-            acc[:, 0:width] += lax.dot_general(
+            more = lax.dot_general(
                 hot[r], spread, (((1,), (1,)), ((), ())), preferred_element_type=F32
             )
+            if low > 0:
+                acc[:, 0:width] += more
+            else:
+                acc[:, 0:width] = more
             return 0
 
-        lax.fori_loop(0, BRICKS, source, 0)
-        for i in range(vectors):
-            for z in range(CZ):
-                part = acc[z * CY * XH : (z + 1) * CY * XH, i * LANES : (i + 1) * LANES]
-                ext[first + i, z + 1, 1 : CY + 1] = part.astype(BF16).reshape(CY, XH, LANES)
-            launch(0, first + i)
+        if low == 0:
+            source(0, 0)
+        else:
+            lax.fori_loop(low, high, source, 0)
+        if high == BRICKS:
+            for i in range(vectors):
+                for z in range(CZ):
+                    part = acc[z * CY * XH : (z + 1) * CY * XH, i * LANES : (i + 1) * LANES]
+                    ext[first + i, z + 1, 1 : CY + 1] = part.astype(BF16).reshape(CY, XH, LANES)
+                launch(0, first + i)
+
+    def bulk(g, low, high):
+        for r in range(low, high):
+            forward(g, r).start()
 
     def convolve(stage, v, z):
         e = stage * (NT + 1) + v
@@ -333,9 +340,8 @@
             device_id_type=MESH,
         )
 
-    def pick(p):
-        def source(i, _):
-            r = BRICKS - 1 - i
+    def pick(p, low, high):
+        def source(r, _):
             fetched = jnp.dot(
                 final[2 * p * LANES : 2 * (p + 1) * LANES, :], hot[r], preferred_element_type=F32
             )
@@ -359,48 +365,64 @@
 
             return 0
 
-        lax.fori_loop(0, BRICKS, source, 0)
+        lax.fori_loop(low, high, source, 0)
+
+    def collect(r, _):
+        for p in range(2):
+            backward(p, r).wait_recv()
+        total[...] += unpack(r)
+        return 0
 
     prepare()
     recv[0] = pack(0)
-    pl.semaphore_wait(gate, len(peers) + len(around))
+
+    def pack_only(r, _):
+        packed[r] = pack(r)
+        return 0
 
     def pack_and_send(r, _):
         packed[r] = pack(r)
+        forward(2, r).start()
         forward(0, r).start()
         return 0
 
-    lax.fori_loop(1, BRICKS, pack_and_send, 0)
-    for g in range(1, len(GROUPS)):
-        for r in range(1, BRICKS):
-            forward(g, r).start()
+    early = 4
+    lax.fori_loop(1, early, pack_only, 0)
+    pl.semaphore_wait(gate, len(peers) + len(around))
+    for r in range(1, early):
+        forward(2, r).start()
+        forward(0, r).start()
+    lax.fori_loop(early, BRICKS, pack_and_send, 0)
+    bulk(1, 1, BRICKS)
+    make_hot(0)
     deposit(0, 0, 1)
+
+    def mark(r, _):
+        forward(2, r).wait_recv()
+        make_hot(r)
+        return 0
+
+    lax.fori_loop(1, BRICKS, mark, 0)
+    deposit(0, 1, 8)
     sweep(0, base_one, 0, 1)
+    sweep(0, tangent_one, 1, 3)
+    deposit(1, 0, 1)
+    deposit(1, 1, 8)
     sweep(1, base_two, 0, 1)
+    sweep(1, tangent_two, 1, 3)
+    sweep(0, tangent_one, 3, 5)
     arrive(2, 0)
     planes(base_three)
-    deposit(1, 1, 2)
-    sweep(0, tangent_one, 1, 3)
-    sweep(1, tangent_two, 1, 3)
-    deposit(2, 3, 2)
     sweep(2, tangent_three, 1, 3)
-    sweep(0, tangent_one, 3, 5)
+    sweep(1, tangent_two, 3, 5)
     sweep(3, tangent_four, 1, 3)
-    pick(0)
-    sweep(1, tangent_two, 3, 5)
+    pick(0, 0, 2)
     sweep(2, tangent_three, 3, 5)
+    pick(0, 2, 8)
     sweep(3, tangent_four, 3, 5)
-    pick(1)
-    total[...] = jnp.zeros_like(total)
-    for p in range(2):
-        unpack(p, 0)
-
-        def collect(r, _):
-            backward(p, r).wait_recv()
-            unpack(p, r)
-            return 0
-
-        lax.fori_loop(1, BRICKS, collect, 0)
+    pick(1, 0, 8)
+    total[...] = unpack(0)
+    lax.fori_loop(1, BRICKS, collect, 0)
     picked[...] = total[...].astype(BF16)
 
     def finish(r, _):
@@ -452,7 +474,7 @@
             pltpu.VMEM((BRICKS, DEPTH, CAP), BF16),
             pltpu.VMEM((BRICKS, ROWS, CAP), BF16),
             pltpu.VMEM((fields, CZ + 2, CY + 2, XH, LANES), BF16),
-            pltpu.VMEM((ROWS, 2 * LANES), F32),
+            pltpu.VMEM((ROWS, 3 * LANES), F32),
             pltpu.VMEM((NT, ROWS, LANES), F32),
             pltpu.VMEM((ROWS, LANES), F32),
             pltpu.VMEM((ROWS, LANES), F32),

time: 144 us -> 115 us (0.80)
  Pallas kernels: 138 us -> 110 us
    pallas_call x1, Pallas kernels: 138 us -> 110 us  [shards(): pl.pallas_call(whole_kernel, name='whole', out_shape=(jax.ShapeDtypeStruc...]
where the time goes in v2:
time: 115 us; the launch traced here: 113 us
  Pallas kernels  110 us (96%)
  other arithmetic  2.93 us (3%)
    pallas_call x1, Pallas kernels, shards(): pl.pallas_call(whole_kernel, name='whole', out_shape=(jax.ShapeDtypeStruc...  110 us
    mul x1, other arithmetic, shards(): return picked.reshape(NT, CH, ATOMS).astype(F32) * tab  2.93 us

profile of v2, /device:TPU:0, one launch (start us, length us, event | category | flops | bytes accessed | tf_op | source)
XLA Modules:
  0.0 113.3 jit_solution(2102451972366541488)
XLA Ops:
  0.0 110.4 %whole.1 = (bf16[256,2048]{1,0:T(8,128)(2,1)}, f32[64,2048]{1,0:T(8,128)}) custom-call(bf16[64,2048]{1,0:T(8,128)(2,1)} %feat.1, bf16[4,64,2048]{2,1,0:T(8,128)(2,1)} %tang.1, s32[1,2048]{1,0:T(1,128)} %bitcast.9, s32[1,2048]{1,0:T(1,128)} %bitcast.10, s32[1,2048]{1,0:T(1,128)} %bitcast.11, f32[8,64]{1,0:T(8,128)} %table.1, f32[3,3,64]{2,1,0:T(4,128)} %taps_one.1, ...), custom_call_target="tpu_custom_call" | custom-call | tf_op jit(solution)/shard_map/whole/pallas_call | solution.py:458
  110.4 2.9 %convert_multiply_fusion = f32[4,64,2048]{2,1,0:T(8,128)} fusion(bf16[4,64,2048]{2,1,0:T(8,128)(2,1)} %bitcast.8, f32[64,2048]{1,0:T(8,128)} %get-tuple-element.8), kind=kLoop, calls=%fused_computation | loop fusion | flops 1048576 | bytes 3670016 | tf_op jit(solution)/shard_map/mul | solution.py:504

commit v3 on v2

--- a/solution.py
+++ b/solution.py
@@ -38,13 +38,17 @@
     return jnp.concatenate([value, value], axis=-1)
 
 
-def whole_kernel(
-    feat, tang, route, cell, sten, table, taps_one, taps_two, point_one, point_two, bias_one, bias_two, readout,
-    picked, tab,
-    data, place_in, place_out, column, slots, packed, recv, hot, ext, acc, t_one, slope, bend, curve,
-    final, send, got, total, taps, mixers, rows3,
-    a_send, a_recv, h_send, h_recv, b_send, b_recv,
-):
+def whole_kernel(*refs):
+    sources, (picked, tab), inputs, rest = refs[:13], refs[13:15], refs[15:28], refs[28:]
+    (
+        feat, tang, route, cell, sten, table, taps_one, taps_two,
+        point_one, point_two, bias_one, bias_two, readout,
+    ) = inputs
+    (
+        data, place_in, place_out, column, slots, packed, recv, hot, ext, acc, t_one, slope, bend, curve,
+        final, send, got, total, taps, mixers, rows3,
+        a_send, a_recv, h_send, h_recv, b_send, b_recv, load_sem,
+    ) = rest
     slab = lax.axis_index("slab")
     place = lax.axis_index("brick")
     x_hi = place % 2
@@ -64,6 +68,14 @@
     gate = pltpu.get_barrier_semaphore()
     for peer in peers + around:
         pl.semaphore_signal(gate, inc=1, device_id=peer, device_id_type=MESH)
+    loads = [
+        pltpu.make_async_copy(source, target, load_sem.at[i])
+        for i, (source, target) in enumerate(zip(sources, inputs))
+    ]
+    for load in loads:
+        load.start()
+    for load in loads:
+        load.wait()
 
     def forward(g, r):
         start, size = GROUPS[g]
@@ -386,7 +398,7 @@
         forward(0, r).start()
         return 0
 
-    early = 4
+    early = 2
     lax.fori_loop(1, early, pack_only, 0)
     pl.semaphore_wait(gate, len(peers) + len(around))
     for r in range(1, early):
@@ -416,9 +428,8 @@
     sweep(2, tangent_three, 1, 3)
     sweep(1, tangent_two, 3, 5)
     sweep(3, tangent_four, 1, 3)
-    pick(0, 0, 2)
     sweep(2, tangent_three, 3, 5)
-    pick(0, 2, 8)
+    pick(0, 0, 8)
     sweep(3, tangent_four, 3, 5)
     pick(1, 0, 8)
     total[...] = unpack(0)
@@ -455,6 +466,11 @@
 ):
     fields = 4 * (NT + 1)
     dma = pltpu.SemaphoreType.DMA
+    operands = (
+        features, tangents, route.reshape(1, ATOMS), cell_local.reshape(1, ATOMS), stencil.reshape(1, ATOMS),
+        stencil_table, taps1, taps2, point1, point2,
+        bias1.reshape(1, CH), bias2.reshape(1, CH), readout.reshape(1, CH),
+    )
     picked, tab = pl.pallas_call(
         whole_kernel,
         name="whole",
@@ -462,9 +478,10 @@
             jax.ShapeDtypeStruct((NT * CH, ATOMS), BF16),
             jax.ShapeDtypeStruct((CH, ATOMS), F32),
         ),
-        in_specs=[VMEM] * 13,
+        in_specs=[pl.BlockSpec(memory_space=pltpu.HBM)] * 13,
         out_specs=(VMEM, VMEM),
-        scratch_shapes=[
+        scratch_shapes=[pltpu.VMEM(value.shape, value.dtype) for value in operands]
+        + [
             pltpu.VMEM((DEPTH, ATOMS), BF16),
             pltpu.VMEM((ATOMS, CAP), BF16),
             pltpu.VMEM((CAP, ATOMS), BF16),
@@ -492,15 +509,12 @@
             dma((fields, 8)),
             dma((2, BRICKS)),
             dma((2, BRICKS)),
+            dma((13,)),
         ],
         compiler_params=pltpu.CompilerParams(
-            collective_id=0, has_side_effects=True, vmem_limit_bytes=60 * 1024 * 1024
+            collective_id=0, has_side_effects=True, vmem_limit_bytes=50 * 1024 * 1024
         ),
-    )(
-        features, tangents, route.reshape(1, ATOMS), cell_local.reshape(1, ATOMS), stencil.reshape(1, ATOMS),
-        stencil_table, taps1, taps2, point1, point2,
-        bias1.reshape(1, CH), bias2.reshape(1, CH), readout.reshape(1, CH),
-    )
+    )(*(pltpu.with_memory_space_constraint(value, pltpu.HBM) for value in operands))
     return picked.reshape(NT, CH, ATOMS).astype(F32) * tab
 
 

time: 115 us -> 110 us (0.957); the launches traced: 113 us -> 109 us
  Pallas kernels: 110 us -> 108 us
  other arithmetic: 2.93 us -> 1.58 us
    pallas_call x1, Pallas kernels: 110 us -> 108 us  [shards(): pl.pallas_call(whole_kernel, name='whole', out_shape=(jax.ShapeDtypeStruc...]
    mul x1, other arithmetic: 2.93 us -> 1.58 us  [shards(): return picked.reshape(NT, CH, ATOMS).astype(F32) * tab]
where the time goes in v3:
time: 110 us; the launch traced here: 109 us
  Pallas kernels  108 us (98%)
  other arithmetic  1.58 us (1%)
    pallas_call x1, Pallas kernels, shards(): pl.pallas_call(whole_kernel, name='whole', out_shape=(jax.ShapeDtypeStruc...  108 us

profile of v3, /device:TPU:0, one launch (start us, length us, event | category | flops | bytes accessed | tf_op | source)
XLA Modules:
  0.0 109.5 jit_solution(2122182579919813283)
XLA Ops:
  0.0 107.9 %whole.1 = (bf16[256,2048]{1,0:T(8,128)(2,1)S(1)}, f32[64,2048]{1,0:T(8,128)S(1)}) custom-call(bf16[64,2048]{1,0:T(8,128)(2,1)} %refs_0_.1, bf16[4,64,2048]{2,1,0:T(8,128)(2,1)} %refs_1_.1, s32[1,2048]{1,0:T(1,128)} %bitcast.9, s32[1,2048]{1,0:T(1,128)} %bitcast.10, s32[1,2048]{1,0:T(1,128)} %bitcast.11, f32[8,64]{1,0:T(8,128)} %refs_5_.1, ...), custom_call_target="tpu_custom_call" | custom-call | tf_op jit(solution)/shard_map/whole/pallas_call | solution.py:474
  107.9 1.6 %convert_multiply_fusion = f32[4,64,2048]{2,1,0:T(8,128)} fusion(bf16[4,64,2048]{2,1,0:T(8,128)(2,1)S(1)} %bitcast.8, f32[64,2048]{1,0:T(8,128)S(1)} %get-tuple-element.8), kind=kLoop, calls=%fused_computation | loop fusion | flops 1048576 | bytes 3670016 | tf_op jit(solution)/shard_map/mul | solution.py:518

commit v4 on v3

--- a/solution.py
+++ b/solution.py
@@ -189,9 +189,10 @@
         for copy in halo(stage, v):
             copy.start()
 
-    def arrive(stage, v):
-        for copy in halo(stage, v):
-            copy.wait_recv()
+    def arrive(stage, v, which):
+        copies = halo(stage, v)
+        for i in which:
+            copies[i].wait_recv()
 
     def split_mask(r):
         low = recv[r, 0:HEAD, :].astype(F32)[1:2, :]
@@ -294,14 +295,17 @@
     def put(stage, v, z, value):
         ext[stage * (NT + 1) + v, z + 1, 1 : CY + 1] = value.astype(BF16).reshape(CY, XH, LANES)
 
-    def planes(body):
-        for z in range(CZ):
+    def planes(stage, v, body):
+        arrive(stage, v, (4, 5))
+        for z in range(1, CZ - 1):
             body(z)
+        arrive(stage, v, (0, 1, 2, 3, 6, 7))
+        body(0)
+        body(CZ - 1)
 
     def sweep(stage, body, low, high):
         def step(v, _):
-            arrive(stage, v)
-            planes(functools.partial(body, v))
+            planes(stage, v, functools.partial(body, v))
             if stage < 3:
                 launch(stage + 1, v)
             return 0
@@ -416,15 +420,15 @@
 
     lax.fori_loop(1, BRICKS, mark, 0)
     deposit(0, 1, 8)
+    deposit(1, 0, 1)
+    deposit(1, 1, 5)
     sweep(0, base_one, 0, 1)
     sweep(0, tangent_one, 1, 3)
-    deposit(1, 0, 1)
-    deposit(1, 1, 8)
+    deposit(1, 5, 8)
     sweep(1, base_two, 0, 1)
     sweep(1, tangent_two, 1, 3)
     sweep(0, tangent_one, 3, 5)
-    arrive(2, 0)
-    planes(base_three)
+    planes(2, 0, base_three)
     sweep(2, tangent_three, 1, 3)
     sweep(1, tangent_two, 3, 5)
     sweep(3, tangent_four, 1, 3)

time: 110 us -> 109 us (level)
  no operation moved by 1% of the time
where the time goes in v4:
time: 109 us
  Pallas kernels  107 us (98%)
  other arithmetic  1.58 us (1%)
    pallas_call x1, Pallas kernels, shards(): pl.pallas_call(whole_kernel, name='whole', out_shape=(jax.ShapeDtypeStruc...  107 us

profile of v4, /device:TPU:0, one launch (start us, length us, event | category | flops | bytes accessed | tf_op | source)
XLA Modules:
  0.0 108.9 jit_solution(12644013854163247006)
XLA Ops:
  0.0 107.3 %whole.1 = (bf16[256,2048]{1,0:T(8,128)(2,1)S(1)}, f32[64,2048]{1,0:T(8,128)S(1)}) custom-call(bf16[64,2048]{1,0:T(8,128)(2,1)} %refs_0_.1, bf16[4,64,2048]{2,1,0:T(8,128)(2,1)} %refs_1_.1, s32[1,2048]{1,0:T(1,128)} %bitcast.9, s32[1,2048]{1,0:T(1,128)} %bitcast.10, s32[1,2048]{1,0:T(1,128)} %bitcast.11, f32[8,64]{1,0:T(8,128)} %refs_5_.1, ...), custom_call_target="tpu_custom_call" | custom-call | tf_op jit(solution)/shard_map/whole/pallas_call | solution.py:478
  107.3 1.6 %convert_multiply_fusion = f32[4,64,2048]{2,1,0:T(8,128)} fusion(bf16[4,64,2048]{2,1,0:T(8,128)(2,1)S(1)} %bitcast.8, f32[64,2048]{1,0:T(8,128)S(1)} %get-tuple-element.8), kind=kLoop, calls=%fused_computation | loop fusion | flops 1048576 | bytes 3670016 | tf_op jit(solution)/shard_map/mul | solution.py:522
